TPU v7x, 32 devices: a whole 2x2x4 slice. The times are simulated.
32 devices in a mesh: groups: 2 (over y), passage: 8 (over z, x), tensor: 2 (over core).
Axes of the slice: x: 2, y: 2, z: 4, core: 2. Of those that a mesh axis runs over, the one named last changes fastest.
Arguments:
- corpus: bfloat16 [96, 256, 1024], P(('groups', 'passage')), parts along dimension 0, may hold values from -6 to 6
- queries: bfloat16 [32, 2048], P(('groups', 'passage'), 'tensor'), parts along dimension 0, may hold values from -180 to 180
- key_weight: bfloat16 [1024, 2048], P('passage', 'tensor'), may hold values from -0.1875 to 0.1875
- value_weight: bfloat16 [1024, 2048], P('passage', 'tensor'), may hold values from -0.1875 to 0.1875
- retrieved: int32 [2, 16], P('groups'), parts along dimension 0, may hold values from 0 to 47, as said below
- placement_map: int32 [96], P('groups'), parts along dimension 0, may hold values from 0 to 47, as said below
- valid_counts: int32 [96], P('groups'), parts along dimension 0, may hold values from 16 to 256
Outputs:
- context: bfloat16 [32, 2048], P(('groups', 'passage'), 'tensor'), parts along dimension 0
There are 2 independent parts, one for each index of `groups`. A program takes and returns all parts, laid end to end along the dimension named above; an argument that names none is the same for every part. Nothing has to cross between parts.
Inputs may be any that keep to these rules, and one draw needn't show every extreme that they name: Each row lists 16 ids; all 16 retrieved ids are distinct. With shard = placement_map[id] // 6, at most 5 retrieved passages lie on one shard, and some shard holds exactly 5. `placement_map`: A permutation of the corpus rows.
All inputs are finite; a program needn't handle non-finite values.
Results may differ from a plain program's by a relative error of at most 0.01.
The roundings to bfloat16 on the way count: a program that leaves them out, or rounds other values in their place, can miss the bound.
Values may be sent and summed in bfloat16 or wider, within the bound.
A program may use at most 64 MiB of HBM per device.

v0:
```python
import jax
import jax.numpy as jnp
from jax import lax
from jax.sharding import PartitionSpec as P

DH = 64
LEN = 256
MOST = 5
QT = 16


def normalize(hidden):
    values32 = hidden.astype(jnp.float32)
    factor = lax.rsqrt(jnp.mean(values32 * values32, axis=-1, keepdims=True) + 1e-06)
    return (values32 * factor).astype(jnp.bfloat16)


def widen(stats):
    return jnp.repeat(stats, DH, axis=-1)


def join_partials(first, second):
    top_one, mass_one, ctx_one = first
    top_two, mass_two, ctx_two = second
    highest = jnp.maximum(top_one, top_two)
    scale_one = jnp.exp(top_one - highest)
    scale_two = jnp.exp(top_two - highest)
    return (
        highest,
        mass_one * scale_one + mass_two * scale_two,
        ctx_one * widen(scale_one) + ctx_two * widen(scale_two),
    )


def on_device(corpus, queries, key_weight, value_weight, retrieved, placement_map, valid_counts):
    shard_index = lax.axis_index("passage")
    corp_rows = corpus.shape[0]
    per_question = retrieved.shape[1]
    total_ret = retrieved.shape[0] * per_question
    flat_ids = retrieved.reshape(total_ret)
    corpus_row = placement_map[flat_ids]
    lengths = valid_counts[flat_ids]
    owned_mask = corpus_row // corp_rows == shard_index
    owner_rank = jnp.cumsum(owned_mask.astype(jnp.int32)) - 1
    slot_iota = jnp.arange(MOST, dtype=jnp.int32)
    selector = (owned_mask[None, :] & (owner_rank[None, :] == slot_iota[:, None])).astype(jnp.int32)
    local_rows = jnp.sum(selector * (corpus_row % corp_rows)[None, :], axis=1)
    slot_lengths = jnp.sum(selector * lengths[None, :], axis=1)
    question_ids = jnp.arange(total_ret, dtype=jnp.int32) // per_question
    slot_question = jnp.sum(selector * question_ids[None, :], axis=1)
    passages = corpus[local_rows]
    normed = normalize(passages).reshape(MOST * LEN, passages.shape[2])
    full_key, full_value = (
        lax.all_gather(key_weight, "passage", axis=0, tiled=True),
        lax.all_gather(value_weight, "passage", axis=0, tiled=True),
    )
    width = key_weight.shape[1]
    heads = width // DH
    key_rows = jnp.dot(normed, full_key, preferred_element_type=jnp.float32).astype(jnp.bfloat16)
    value_rows = jnp.dot(normed, full_value, preferred_element_type=jnp.float32).astype(
        jnp.bfloat16
    )
    key_rows = key_rows.reshape(MOST, LEN, heads, DH)
    value_rows = value_rows.reshape(MOST, LEN, heads, DH)
    all_queries = lax.all_gather(queries, "passage", axis=0, tiled=True)
    query_total = all_queries.shape[0]
    best_score = jnp.full((query_total, heads), -1e30, jnp.float32)
    row_total = jnp.zeros((query_total, heads), jnp.float32)
    context_sum = jnp.zeros((query_total, width), jnp.float32)
    positions = jnp.arange(LEN, dtype=jnp.int32)
    scaling = DH ** (-0.5)
    for number in range(MOST):
        first_row = slot_question[number] * QT
        block = lax.dynamic_slice_in_dim(all_queries, first_row, QT, 0).reshape(QT, heads, DH)
        scores = (
            jnp.einsum("thd,lhd->htl", block, key_rows[number], preferred_element_type=jnp.float32)
            * scaling
        )
        live_mask = (positions < slot_lengths[number])[None, None, :]
        scores = jnp.where(live_mask, scores, jnp.float32(-1e30))
        top_score = jnp.max(scores, axis=-1)
        weights = jnp.where(live_mask, jnp.exp(scores - top_score[..., None]), jnp.float32(0.0))
        row_mass = jnp.sum(weights, axis=-1)
        partial_ctx = jnp.einsum(
            "htl,lhd->thd",
            weights.astype(jnp.bfloat16),
            value_rows[number],
            preferred_element_type=jnp.float32,
        ).reshape(QT, width)
        old_state = (
            lax.dynamic_slice_in_dim(best_score, first_row, QT, 0),
            lax.dynamic_slice_in_dim(row_total, first_row, QT, 0),
            lax.dynamic_slice_in_dim(context_sum, first_row, QT, 0),
        )
        new_top, new_mass, new_ctx = join_partials(
            old_state, (top_score.T, row_mass.T, partial_ctx)
        )
        best_score = lax.dynamic_update_slice_in_dim(best_score, new_top, first_row, 0)
        row_total = lax.dynamic_update_slice_in_dim(row_total, new_mass, first_row, 0)
        context_sum = lax.dynamic_update_slice_in_dim(context_sum, new_ctx, first_row, 0)
    global_top = lax.pmax(best_score, "passage")
    rescale = jnp.exp(best_score - global_top)
    own_mass, own_ctx = (
        lax.psum_scatter(row_total * rescale, "passage", scatter_dimension=0, tiled=True),
        lax.psum_scatter(context_sum * widen(rescale), "passage", scatter_dimension=0, tiled=True),
    )
    return (own_ctx / widen(own_mass)).astype(jnp.bfloat16)


def solution(mesh):
    in_specs = (
        P(("groups", "passage"), None, None),
        P(("groups", "passage"), "tensor"),
        P("passage", "tensor"),
        P("passage", "tensor"),
        P("groups", None),
        P("groups"),
        P("groups"),
    )
    out_specs = P(("groups", "passage"), "tensor")
    return jax.shard_map(
        on_device, mesh=mesh, in_specs=in_specs, out_specs=out_specs, check_vma=False
    )
```

profile of v0, /device:TPU:0, one launch (start us, length us, event | category | flops | bytes accessed | tf_op | source)
XLA Modules:
  0.0 196.4 jit_solution(11612404778578878747)
XLA Ops:
  6.5 0.0 copy-start
  6.5 0.7 all-gather.4.cloned.1.call-update
  7.3 0.0 all-gather.6.cloned.1.call-start
  7.3 0.7 all-gather.6.cloned.1.call-update
  8.0 0.0 all-reduce.4.cloned.1.call-start
  8.1 0.7 fusion.84
  8.7 1.3 gather_fusion
  10.1 0.1 copy.32
  10.2 0.1 copy.33
  10.3 0.1 add_reduce_fusion
  10.4 1.3 gather_fusion.1
  11.7 0.2 select_reduce_fusion.1
  11.9 0.0 copy-done
  11.9 2.4 %gather_fusion.2 = bf16[5,256,1024]{2,1,0:T(8,128)(2,1)} fusion(bf16[6,256,1024]{2,1,0:T(8,128)(2,1)S(1)} %copy-done, s32[1024]{0:T(1024)S(1)} %pad_clamp_fusion), kind=kCustom, calls=%fused_computation.2 | custom fusion | bytes 5242900 | tf_op jit(solution)/shard_map/gather | solution.py:51
  14.3 2.3 %multiply_reduce_fusion = f32[5,256]{1,0:T(8,128)S(1)} fusion(bf16[5,256,1024]{2,1,0:T(8,128)(2,1)} %gather_fusion.2), kind=kLoop, calls=%fused_computation.5 | loop fusion | flops 3930880 | bytes 2626560 | tf_op jit(solution)/shard_map/reduce_sum | solution.py:14
  16.7 0.7 fusion.99
  17.3 0.7 iota_compare_fusion.4
  18.0 32.4 %all-gather = bf16[8,2,1024]{2,1,0:T(2,128)(2,1)S(1)} all-gather(bf16[1,2,1024]{2,1,0:T(2,128)(2,1)S(1)} %bitcast.194), channel_id=1, replica_groups=mesh['groups'=2,'passage'=8,'tensor'=2] {'passage'}, dimensions={0}, use_global_device_ids=true | all-gather | bytes 36864 | tf_op jit(solution)/shard_map/all_gather | solution.py:65
  50.4 0.1 reshape.255
  50.6 0.6 dynamic-slice
  51.9 0.7 iota_compare_fusion.5
  52.5 0.6 iota_compare_fusion.2
  53.2 0.6 iota_compare_fusion.3
  53.8 0.6 iota_compare_fusion.1
  54.4 0.0 copy-start.5
  54.4 3.8 %fusion = bf16[1280,1024]{1,0:T(8,128)(2,1)} fusion(f32[1280]{0:T(1024)S(1)} %rsqrt.12, bf16[5,256,1024]{2,1,0:T(8,128)(2,1)} %gather_fusion.2), kind=kLoop, calls=%fused_computation.4 | loop fusion | flops 3932160 | bytes 5248000 | tf_op jit(solution)/shard_map/convert_element_type | solution.py:15
  58.2 3.6 %all-gather.4.cloned.1.call-done = bf16[1024,1024]{1,0:T(8,128)(2,1)} async-done(((bf16[128,1024]{1,0:T(8,128)(2,1)}), bf16[1024,1024]{1,0:T(8,128)(2,1)}) %all-gather.4.cloned.1.call-update) | async-done | bytes 2097168 | tf_op jit(solution)/shard_map/all_gather | solution.py:54
  61.8 5.3 %convolution_convert_fusion.1 = bf16[1280,1024]{0,1:T(8,128)(2,1)S(1)} fusion(bf16[1280,1024]{1,0:T(8,128)(2,1)} %fusion, bf16[1024,1024]{1,0:T(8,128)(2,1)} %all-gather.4.cloned.1.call-done), kind=kOutput, calls=%fused_computation.7 | convolution fusion | flops 2685665280 | bytes 7340032 | tf_op jit(solution)/shard_map/dot_general | solution.py:59
  67.1 0.2 fusion.98
  67.3 0.9 fusion.104
  68.2 0.9 fusion.100
  69.1 0.3 fusion.102
  69.4 0.9 fusion.103
  70.3 0.9 fusion.101
  71.2 19.5 %pmax.7 = f32[16,16]{0,1:T(8,128)S(1)} all-reduce(f32[16,16]{0,1:T(8,128)S(1)} %get-tuple-element.17), channel_id=1, replica_groups=mesh['groups'=2,'passage'=8,'tensor'=2] {'passage'}, use_global_device_ids=true, to_apply=%region_9.10 | all-reduce | flops 256 | bytes 2048 | tf_op jit(solution)/shard_map/pmax | solution.py:101
  90.7 1.1 fusion.34
  91.8 20.2 %all-gather.6.cloned.1.call-done = bf16[1024,1024]{1,0:T(8,128)(2,1)} async-done(((bf16[128,1024]{1,0:T(8,128)(2,1)}), bf16[1024,1024]{1,0:T(8,128)(2,1)}) %all-gather.6.cloned.1.call-update) | async-done | bytes 2097168 | tf_op jit(solution)/shard_map/all_gather | solution.py:55
  112.0 5.3 %convolution_convert_fusion = bf16[1280,1024]{0,1:T(8,128)(2,1)S(1)} fusion(bf16[1280,1024]{1,0:T(8,128)(2,1)} %fusion, bf16[1024,1024]{1,0:T(8,128)(2,1)} %all-gather.6.cloned.1.call-done), kind=kOutput, calls=%fused_computation.6 | convolution fusion | flops 2685665280 | bytes 7340032 | tf_op jit(solution)/shard_map/dot_general | solution.py:60
  117.4 0.0 copy-start.2
  117.4 0.0 copy-start.4
  117.4 0.0 copy-start.3
  117.4 0.2 fusion.97
  117.6 0.7 copy-done.2
  118.3 0.1 copy-done.4
  118.4 0.2 fusion.26
  118.7 0.0 copy-start.1
  118.7 0.0 copy-start.6
  118.7 0.2 fusion.30
  119.0 0.3 fusion.25
  119.3 0.3 fusion.22
  119.6 0.3 fusion.19
  119.9 0.3 fusion.16
  120.3 0.0 copy-done.6
  120.3 0.3 fusion.13
  120.6 0.1 copy.40
  120.7 0.7 reshape.298
  121.4 0.0 all-reduce.4.cloned.1.call-update
  121.4 19.2 %all-reduce.1 = f32[16,16]{0,1:T(8,128)S(1)} all-reduce(f32[16,16]{0,1:T(8,128)S(1)} %get-tuple-element.34), channel_id=3, replica_groups=mesh['groups'=2,'passage'=8,'tensor'=2] {'passage'}, use_global_device_ids=true, to_apply=%region_16.17.clone | all-reduce | flops 256 | bytes 2048
  140.6 0.1 constant_dynamic-slice_fusion
  140.7 0.1 copy.41
  140.8 0.1 broadcast_in_dim.147
  140.9 0.1 reshape.260
  141.0 47.6 %all-reduce.4.cloned.1.call-done = f32[16,1024]{1,0:T(8,128)} async-done(((f32[16,1024]{1,0:T(8,128)}), f32[16,1024]{1,0:T(8,128)}) %all-reduce.4.cloned.1.call-update) | async-done | bytes 65552
  188.6 1.4 fusion.81
  (19 shorter events, 0.2 us)
Async XLA Ops:
  6.5 5.4 %copy-start = (bf16[6,256,1024]{2,1,0:T(8,128)(2,1)S(1)}, bf16[6,256,1024]{2,1,0:T(8,128)(2,1)}, u32[]{:S(2)}) copy-start(bf16[6,256,1024]{2,1,0:T(8,128)(2,1)} %param.7) | copy-start | bytes 9437188
  6.5 55.3 %all-gather.4.cloned.1.call-start = ((), (), s32[]{:S(2)}) async-start(), calls=%async_computation | async-start | bytes 2359296 | tf_op jit(solution)/shard_map/all_gather | solution.py:54
  7.3 104.8 %all-gather.6.cloned.1.call-start = ((), (), s32[]{:S(2)}) async-start(), calls=%async_computation.1 | async-start | bytes 2359296 | tf_op jit(solution)/shard_map/all_gather | solution.py:55
  8.0 180.6 %all-reduce.4.cloned.1.call-start = ((), (), s32[]{:S(2)}) async-start(), calls=%async_computation.2 | async-start | bytes 131072
  14.3 3.7 %copy-start.7 = (bf16[2,1024]{1,0:T(2,128)(2,1)S(1)}, bf16[2,1024]{1,0:T(2,128)(2,1)}, u32[]{:S(2)}) copy-start(bf16[2,1024]{1,0:T(2,128)(2,1)} %param.8) | copy-start | bytes 12292
  14.3 36.3 %copy-start.8 = (u32[32]{0:T(128)S(1)}, u32[32]{0:T(128)}, u32[]{:S(2)}) copy-start(u32[32]{0:T(128)} %constant.68) | copy-start | bytes 388
  54.4 36.3 %copy-start.5 = (pred[256]{0:T(512)(128)(4,1)}, pred[256]{0:T(512)(128)(4,1)S(1)}, u32[]{:S(2)}) copy-start(pred[256]{0:T(512)(128)(4,1)S(1)} %iota_compare_fusion.1) | copy-start | bytes 772
  117.4 1.0 copy-start.2
  117.4 1.0 copy-start.4
  117.4 1.3 copy-start.3
  118.7 1.6 copy-start.1
  118.7 1.6 copy-start.6
Sparse Core Ops, SparseCore 0:
  9.5 52.2 all-gather.3
  63.9 48.0 all-gather.5
  121.5 66.9 all-reduce.3
where the time goes:
time: 197 us; the launch traced here: 196 us
  waiting for transfers between devices  72.9 us (37%)
  blocking collectives  71.1 us (36%)
  matrix products  16.1 us (8%)
  between operations  14.1 us (7%)
  other arithmetic  13.3 us (7%)
  local copies, waits for them, and re-layouts  8.89 us (5%)
    unnamed x4, waiting for transfers between devices  49 us
    all_gather x1, blocking collectives, on_device(): all_queries = lax.all_gather(queries, 'passage', axis=0, tiled=True)  32.4 us
    all_gather x1, waiting for transfers between devices, on_device(): lax.all_gather(value_weight, 'passage', axis=0, tiled=True)  20.2 us
    pmax x1, blocking collectives, on_device(): global_top = lax.pmax(best_score, 'passage')  19.5 us
    unnamed x1, blocking collectives  19.2 us
    dot_general x1, matrix products, on_device(): jnp.dot(normed, full_key, preferred_element_type=jnp.float32)  5.32 us
    dot_general x1, matrix products, on_device(): jnp.dot(normed, full_value, preferred_element_type=jnp.float32)  5.31 us
  transfers between devices with their start and end apart: 3, of which 3 were waited for; matrix products, arithmetic and copies ran while one was open for 14% of the time, Pallas kernels for 0%

commit v1 on v0

--- a/solution.py
+++ b/solution.py
@@ -1,6 +1,8 @@
 import jax
 import jax.numpy as jnp
 from jax import lax
+from jax.experimental import pallas as pl
+from jax.experimental.pallas import tpu as pltpu
 from jax.sharding import PartitionSpec as P
 
 DH = 64
@@ -107,6 +109,369 @@
     return (own_ctx / widen(own_mass)).astype(jnp.bfloat16)
 
 
+MESH = pl.DeviceIdType.MESH
+
+
+def reader_kernel(
+    ids_ref,
+    place_ref,
+    count_ref,
+    corpus_ref,
+    query_ref,
+    key_ref,
+    value_ref,
+    out_ref,
+    tokens,
+    normed,
+    weights,
+    query_in,
+    query_all,
+    query_wide,
+    exp_rows,
+    stats,
+    partial_out,
+    partial_in,
+    w_send,
+    w_recv,
+    q_send,
+    q_recv,
+    s_send,
+    s_recv,
+    c_send,
+    c_recv,
+    local_sem,
+):
+    rows_here, length, width_in = corpus_ref.shape
+    shard_rows, width = key_ref.shape
+    half = shard_rows // 2
+    heads = width // DH
+    per_question = ids_ref.shape[1]
+    group = lax.axis_index("groups")
+    shard = lax.axis_index("passage")
+    z = shard // 2
+    x = shard % 2
+    z1 = z + 1 - 2 * (z % 2)
+    z2 = (z + 2) % 4
+    z3 = 3 - z
+    xo = 1 - x
+    go = 1 - group
+    at_x = {"passage": z * 2 + xo}
+    at_y = {"groups": go}
+
+    barrier = pltpu.get_barrier_semaphore()
+    for step in range(1, 8):
+        peer = (shard + step) % 8
+        pl.semaphore_signal(barrier, inc=1, device_id={"passage": peer}, device_id_type=MESH)
+    pl.semaphore_signal(barrier, inc=1, device_id=at_y, device_id_type=MESH)
+
+    corpus_copies = []
+    for row in range(rows_here):
+        copy = pltpu.make_async_copy(corpus_ref.at[row], tokens.at[row], local_sem.at[row])
+        copy.start()
+        corpus_copies.append(copy)
+    place_copies = []
+    for which, ref in ((0, key_ref), (1, value_ref)):
+        start = pl.multiple_of(shard * shard_rows, shard_rows)
+        copy = pltpu.make_async_copy(
+            ref, weights.at[which, pl.ds(start, shard_rows)], local_sem.at[rows_here + which]
+        )
+        copy.start()
+        place_copies.append(copy)
+    own_query = pltpu.make_async_copy(
+        query_ref, query_in.at[shard], local_sem.at[rows_here + 2]
+    )
+    own_query.start()
+    pl.semaphore_wait(barrier, 8)
+
+    def region(which, zz, xx, part):
+        base = (zz * 2 + xx) * shard_rows
+        if part is None:
+            return weights.at[which, pl.ds(pl.multiple_of(base, shard_rows), shard_rows)]
+        return weights.at[which, pl.ds(pl.multiple_of(base + part * half, half), half)]
+
+    def send(which, number, source, target, device):
+        copy = pltpu.make_async_remote_copy(
+            src_ref=source,
+            dst_ref=target,
+            send_sem=w_send.at[which, number],
+            recv_sem=w_recv.at[which, number],
+            device_id=device,
+            device_id_type=MESH,
+        )
+        copy.start()
+        sent.append(copy)
+
+    def landed(which, number, target):
+        pltpu.make_async_remote_copy(
+            src_ref=target,
+            dst_ref=target,
+            send_sem=w_send.at[which, number],
+            recv_sem=w_recv.at[which, number],
+            device_id=at_x,
+            device_id_type=MESH,
+        ).wait_recv()
+
+    sent = []
+    for step in range(1, 8):
+        peer = (shard + step) % 8
+        copy = pltpu.make_async_remote_copy(
+            src_ref=query_ref,
+            dst_ref=query_in.at[shard],
+            send_sem=q_send.at[step],
+            recv_sem=q_recv.at[step],
+            device_id={"passage": peer},
+            device_id_type=MESH,
+        )
+        copy.start()
+        sent.append(copy)
+
+    for which, ref in ((0, key_ref), (1, value_ref)):
+        mine = ref.at[pl.ds(pl.multiple_of(group * half, half), half)]
+        send(which, 0, ref, region(which, z, x, None), {"passage": z1 * 2 + x})
+        send(which, 3, ref, region(which, z, x, None), at_x)
+        send(which, 1, mine, region(which, z, x, group), {"passage": z2 * 2 + x})
+        send(which, 2, mine, region(which, z, x, group), {"passage": z3 * 2 + x})
+
+    def forward(which, number):
+        if number == 0:
+            landed(which, 0, region(which, z1, x, None))
+            piece = region(which, z1, x, group)
+            send(which, 4, piece, piece, at_x)
+        elif number in (1, 2):
+            zz = (z2, z3)[number - 1]
+            piece = region(which, zz, x, group)
+            landed(which, number, piece)
+            send(which, 4 + number, piece, piece, at_x)
+            send(which, 6 + number, piece, piece, at_y)
+        else:
+            zz = (z1, z2, z3)[number - 4]
+            piece = region(which, zz, xo, group)
+            landed(which, number, piece)
+            send(which, 5 + number, piece, piece, at_y)
+
+    def last_pieces(which):
+        landed(which, 3, region(which, z, xo, None))
+        landed(which, 7, region(which, z2, x, go))
+        landed(which, 8, region(which, z3, x, go))
+        landed(which, 9, region(which, z1, xo, go))
+        landed(which, 10, region(which, z2, xo, go))
+        landed(which, 11, region(which, z3, xo, go))
+
+    def norm(row):
+        corpus_copies[row].wait()
+        values32 = tokens[row].astype(jnp.float32)
+        factor = lax.rsqrt(jnp.mean(values32 * values32, axis=-1, keepdims=True) + 1e-06)
+        normed[row] = (values32 * factor).astype(jnp.bfloat16)
+
+    norm(0)
+    norm(1)
+    forward(0, 0)
+    norm(2)
+    forward(0, 1)
+    forward(0, 2)
+    norm(3)
+    forward(0, 4)
+    forward(1, 0)
+    norm(4)
+    forward(0, 5)
+    forward(0, 6)
+    forward(1, 1)
+    forward(1, 2)
+    norm(5)
+
+    lengths = [jnp.int32(0) for _ in range(rows_here)]
+    for number in range(per_question):
+        name = ids_ref[0, number]
+        place = place_ref[name] - shard * rows_here
+        count = count_ref[name]
+        lengths = [
+            kept + jnp.where(place == row, count, 0) for row, kept in enumerate(lengths)
+        ]
+
+    own_query.wait()
+    for step in range(1, 8):
+        origin = (shard + 8 - step) % 8
+        pltpu.make_async_remote_copy(
+            src_ref=query_ref,
+            dst_ref=query_in.at[origin],
+            send_sem=q_send.at[step],
+            recv_sem=q_recv.at[step],
+            device_id=at_x,
+            device_id_type=MESH,
+        ).wait_recv()
+    for number in range(8):
+        query_all[2 * number : 2 * number + 2, :] = query_in[number].astype(jnp.float32)
+    block = jnp.concatenate([query_all[...]] * heads, axis=0)
+    row_head = lax.broadcasted_iota(jnp.int32, (heads * QT, width), 0) // QT
+    col_head = lax.broadcasted_iota(jnp.int32, (heads * QT, width), 1) // DH
+    query_wide[...] = jnp.where(row_head == col_head, block, 0.0).astype(jnp.bfloat16)
+
+    forward(1, 4)
+    forward(1, 5)
+    forward(1, 6)
+    place_copies[0].wait()
+    last_pieces(0)
+
+    scaling = DH ** (-0.5)
+    positions = lax.broadcasted_iota(jnp.int32, (length, heads * QT), 0)
+    tops, masses = [], []
+    for row in range(rows_here):
+        key_rows = jnp.dot(
+            normed[row], weights[0], preferred_element_type=jnp.float32
+        ).astype(jnp.bfloat16)
+        scores = (
+            lax.dot_general(
+                key_rows,
+                query_wide[...],
+                (((1,), (1,)), ((), ())),
+                preferred_element_type=jnp.float32,
+            )
+            * scaling
+        )
+        live = positions < lengths[row]
+        scores = jnp.where(live, scores, jnp.float32(-1e30))
+        top = jnp.max(scores, axis=0, keepdims=True)
+        exps = jnp.where(live, jnp.exp(scores - top), jnp.float32(0.0))
+        masses.append(jnp.sum(exps, axis=0, keepdims=True))
+        tops.append(top)
+        exp_rows[row] = exps.astype(jnp.bfloat16)
+    peak_here = tops[0]
+    for top in tops[1:]:
+        peak_here = jnp.maximum(peak_here, top)
+    mass_here = masses[0] * jnp.exp(tops[0] - peak_here)
+    for top, mass in zip(tops[1:], masses[1:]):
+        mass_here = mass_here + mass * jnp.exp(top - peak_here)
+    stats[shard] = jnp.concatenate([peak_here, mass_here], axis=0)
+    for step in range(1, 8):
+        peer = (shard + step) % 8
+        copy = pltpu.make_async_remote_copy(
+            src_ref=stats.at[shard],
+            dst_ref=stats.at[shard],
+            send_sem=s_send.at[step],
+            recv_sem=s_recv.at[step],
+            device_id={"passage": peer},
+            device_id_type=MESH,
+        )
+        copy.start()
+        sent.append(copy)
+    for step in range(1, 8):
+        origin = (shard + 8 - step) % 8
+        pltpu.make_async_remote_copy(
+            src_ref=stats.at[origin],
+            dst_ref=stats.at[origin],
+            send_sem=s_send.at[step],
+            recv_sem=s_recv.at[step],
+            device_id=at_x,
+            device_id_type=MESH,
+        ).wait_recv()
+    peak = stats[0, 0:1, :]
+    for number in range(1, 8):
+        peak = jnp.maximum(peak, stats[number, 0:1, :])
+    total = jnp.zeros_like(peak)
+    for number in range(8):
+        total = total + stats[number, 1:2, :] * jnp.exp(stats[number, 0:1, :] - peak)
+    factors = [jnp.exp(top - peak) / total for top in tops]
+    factors += [jnp.zeros_like(peak)] * (8 - rows_here)
+    factors = jnp.transpose(jnp.concatenate(factors, axis=0))
+    context = jnp.zeros((heads * QT, width_in), jnp.float32)
+    for row in range(rows_here):
+        context = context + factors[:, row : row + 1] * lax.dot_general(
+            exp_rows[row],
+            normed[row],
+            (((0,), (0,)), ((), ())),
+            preferred_element_type=jnp.float32,
+        )
+    context = context.astype(jnp.bfloat16)
+
+    place_copies[1].wait()
+    last_pieces(1)
+    mixed = jnp.dot(context, weights[1], preferred_element_type=jnp.float32)
+    mixed = jnp.where(row_head == col_head, mixed, 0.0)
+    summed = mixed[0:QT]
+    for head in range(1, heads):
+        summed = summed + mixed[head * QT : (head + 1) * QT]
+    for number in range(8):
+        partial_out[number] = summed[2 * number : 2 * number + 2]
+    for step in range(1, 8):
+        peer = (shard + step) % 8
+        copy = pltpu.make_async_remote_copy(
+            src_ref=partial_out.at[peer],
+            dst_ref=partial_in.at[shard],
+            send_sem=c_send.at[step],
+            recv_sem=c_recv.at[step],
+            device_id={"passage": peer},
+            device_id_type=MESH,
+        )
+        copy.start()
+        sent.append(copy)
+    result = partial_out[shard]
+    for step in range(1, 8):
+        origin = (shard + 8 - step) % 8
+        pltpu.make_async_remote_copy(
+            src_ref=partial_out.at[origin],
+            dst_ref=partial_in.at[origin],
+            send_sem=c_send.at[step],
+            recv_sem=c_recv.at[step],
+            device_id=at_x,
+            device_id_type=MESH,
+        ).wait_recv()
+        result = result + partial_in[origin]
+    out_ref[...] = result.astype(jnp.bfloat16)
+    for copy in sent:
+        copy.wait_send()
+
+
+def one_question(corpus, queries, key_weight, value_weight, retrieved, placement_map, valid_counts):
+    rows_here, length, width_in = corpus.shape
+    shard_rows, width = key_weight.shape
+    lanes = width // DH * QT
+    smem = pl.BlockSpec(memory_space=pltpu.SMEM)
+    anywhere = pl.BlockSpec(memory_space=pl.ANY)
+    vmem = pl.BlockSpec(memory_space=pltpu.VMEM)
+    dma = pltpu.SemaphoreType.DMA
+    return pl.pallas_call(
+        reader_kernel,
+        out_shape=jax.ShapeDtypeStruct(queries.shape, jnp.bfloat16),
+        in_specs=[smem, smem, smem, anywhere, anywhere, anywhere, anywhere],
+        out_specs=vmem,
+        scratch_shapes=[
+            pltpu.VMEM(corpus.shape, jnp.bfloat16),
+            pltpu.VMEM(corpus.shape, jnp.bfloat16),
+            pltpu.VMEM((2, 8 * shard_rows, width), jnp.bfloat16),
+            pltpu.VMEM((8, 2, width), jnp.bfloat16),
+            pltpu.VMEM((QT, width), jnp.float32),
+            pltpu.VMEM((lanes, width), jnp.bfloat16),
+            pltpu.VMEM((rows_here, length, lanes), jnp.bfloat16),
+            pltpu.VMEM((8, 2, lanes), jnp.float32),
+            pltpu.VMEM((8, 2, width), jnp.float32),
+            pltpu.VMEM((8, 2, width), jnp.float32),
+            dma((2, 12)),
+            dma((2, 12)),
+            dma((8,)),
+            dma((8,)),
+            dma((8,)),
+            dma((8,)),
+            dma((8,)),
+            dma((8,)),
+            dma((rows_here + 3,)),
+        ],
+        compiler_params=pltpu.CompilerParams(
+            collective_id=0, has_side_effects=True, vmem_limit_bytes=48 * 1024 * 1024
+        ),
+    )(retrieved, placement_map, valid_counts, corpus, queries, key_weight, value_weight)
+
+
+def route(*args):
+    corpus, queries, key_weight, value_weight, retrieved, placement_map, valid_counts = args
+    small = (
+        lax.axis_size("groups") == 2
+        and lax.axis_size("passage") == 8
+        and retrieved.shape[0] == 1
+        and queries.shape[0] == 2
+    )
+    return one_question(*args) if small else on_device(*args)
+
+
 def solution(mesh):
     in_specs = (
         P(("groups", "passage"), None, None),
@@ -119,5 +484,5 @@
     )
     out_specs = P(("groups", "passage"), "tensor")
     return jax.shard_map(
-        on_device, mesh=mesh, in_specs=in_specs, out_specs=out_specs, check_vma=False
-    )
+        route, mesh=mesh, in_specs=in_specs, out_specs=out_specs, check_vma=False
+    )

time: 197 us -> 61.8 us (0.31)
  waiting for transfers between devices: 72.9 us -> 0 us
  blocking collectives: 71.1 us -> 0 us
  Pallas kernels: 0 us -> 54.5 us
  matrix products: 16.1 us -> 0 us
  between operations: 14.1 us -> 0.02 us
  other arithmetic: 13.3 us -> 0 us
    pallas_call x0 -> x1, Pallas kernels: none -> 54.5 us  [one_question(): pl.pallas_call(reader_kernel, out_shape=jax.ShapeDtypeStruct(queries.shap...]
    unnamed x4 -> x0, waiting for transfers between devices: 49 us -> none
    all_gather x1 -> x0, blocking collectives: 32.4 us -> none  [on_device(): all_queries = lax.all_gather(queries, 'passage', axis=0, tiled=True)]
    all_gather x2 -> x0, waiting for transfers between devices: 23.9 us -> none  [the longest x1 20.2 us: on_device(): lax.all_gather(value_weight, 'passage', axis=0, tiled=True)]
    pmax x1 -> x0, blocking collectives: 19.5 us -> none  [on_device(): global_top = lax.pmax(best_score, 'passage')]
    unnamed x1 -> x0, blocking collectives: 19.2 us -> none
    dot_general x12 -> x0, matrix products: 16.1 us -> none  [the longest x1 5.32 us: on_device(): jnp.dot(normed, full_key, preferred_element_type=jnp.float32)]
    unnamed x20 -> x15, local copies, waits for them, and re-layouts: 1.58 us -> 7.03 us
  transfers between devices with their start and end apart: 3 -> 0, of which waited for: 3 -> 0; matrix products, arithmetic and copies ran while one was open for 14% -> 0% of each run, Pallas kernels for 0% -> 0%
where the time goes in v1:
time: 61.8 us; the launch traced here: 61.5 us
  Pallas kernels  54.5 us (88%)
  local copies, waits for them, and re-layouts  7.03 us (11%)
    pallas_call x1, Pallas kernels, one_question(): pl.pallas_call(reader_kernel, out_shape=jax.ShapeDtypeStruct(queries.shap...  54.5 us
    unnamed x15, local copies, waits for them, and re-layouts  7.03 us

profile of v1, /device:TPU:0, one launch (start us, length us, event | category | flops | bytes accessed | tf_op | source)
XLA Modules:
  0.0 61.5 jit_solution(5015133376692450472)
XLA Ops:
  0.0 0.0 copy-start
  0.0 1.9 %copy-done = bf16[6,256,1024]{2,1,0:T(8,128)(2,1)S(1)} copy-done((bf16[6,256,1024]{2,1,0:T(8,128)(2,1)S(1)}, bf16[6,256,1024]{2,1,0:T(8,128)(2,1)}, u32[]{:S(2)}) %copy-start) | copy-done | bytes 3145752
  1.9 0.0 copy-start.1
  1.9 0.9 %copy-done.1 = bf16[128,1024]{1,0:T(8,128)(2,1)S(1)} copy-done((bf16[128,1024]{1,0:T(8,128)(2,1)S(1)}, bf16[128,1024]{1,0:T(8,128)(2,1)}, u32[]{:S(2)}) %copy-start.1) | copy-done | bytes 262168
  2.8 0.0 copy-start.2
  2.8 0.9 %copy-done.2 = bf16[128,1024]{1,0:T(8,128)(2,1)S(1)} copy-done((bf16[128,1024]{1,0:T(8,128)(2,1)S(1)}, bf16[128,1024]{1,0:T(8,128)(2,1)}, u32[]{:S(2)}) %copy-start.2) | copy-done | bytes 262168
  3.8 0.0 copy-start.3
  3.8 0.7 %copy-done.3 = bf16[2,1024]{1,0:T(2,128)(2,1)S(1)} copy-done((bf16[2,1024]{1,0:T(2,128)(2,1)S(1)}, bf16[2,1024]{1,0:T(2,128)(2,1)}, u32[]{:S(2)}) %copy-start.3) | copy-done | bytes 4120
  4.5 0.0 copy-start.4
  4.5 0.7 %copy-done.4 = s32[1,16]{1,0:T(1,128)S(1)} copy-done((s32[1,16]{1,0:T(1,128)S(1)}, s32[1,16]{1,0:T(1,128)}, u32[]{:S(2)}) %copy-start.4) | copy-done | bytes 88
  5.1 0.0 copy-start.5
  5.1 0.7 %copy-done.5 = s32[48]{0:T(128)S(1)} copy-done((s32[48]{0:T(128)S(1)}, s32[48]{0:T(128)}, u32[]{:S(2)}) %copy-start.5) | copy-done | bytes 216
  5.8 0.0 copy-start.6
  5.8 0.7 %copy-done.6 = s32[48]{0:T(128)S(1)} copy-done((s32[48]{0:T(128)S(1)}, s32[48]{0:T(128)}, u32[]{:S(2)}) %copy-start.6) | copy-done | bytes 216
  6.4 54.5 %shard_map.73 = bf16[2,1024]{1,0:T(2,128)(2,1)S(1)} custom-call(s32[1,16]{1,0:T(1,128)S(1)} %copy-done.4, s32[48]{0:T(128)S(1)} %copy-done.5, s32[48]{0:T(128)S(1)} %copy-done.6, bf16[6,256,1024]{2,1,0:T(8,128)(2,1)S(1)} %copy-done, bf16[2,1024]{1,0:T(2,128)(2,1)S(1)} %copy-done.3, bf16[128,1024]{1,0:T(8,128)(2,1)S(1)} %copy-done.1, ...), custom_call_target="tpu_custom_call" | custom-call | tf_op jit(solution)/shard_map/pallas_call | solution.py:432
  60.9 0.6 copy.9
Async XLA Ops:
  0.0 1.9 %copy-start = (bf16[6,256,1024]{2,1,0:T(8,128)(2,1)S(1)}, bf16[6,256,1024]{2,1,0:T(8,128)(2,1)}, u32[]{:S(2)}) copy-start(bf16[6,256,1024]{2,1,0:T(8,128)(2,1)} %corpus_ref.1) | copy-start | bytes 9437188
  1.9 0.9 %copy-start.1 = (bf16[128,1024]{1,0:T(8,128)(2,1)S(1)}, bf16[128,1024]{1,0:T(8,128)(2,1)}, u32[]{:S(2)}) copy-start(bf16[128,1024]{1,0:T(8,128)(2,1)} %key_ref.1) | copy-start | bytes 786436
  2.8 0.9 %copy-start.2 = (bf16[128,1024]{1,0:T(8,128)(2,1)S(1)}, bf16[128,1024]{1,0:T(8,128)(2,1)}, u32[]{:S(2)}) copy-start(bf16[128,1024]{1,0:T(8,128)(2,1)} %value_ref.1) | copy-start | bytes 786436
  3.8 0.7 %copy-start.3 = (bf16[2,1024]{1,0:T(2,128)(2,1)S(1)}, bf16[2,1024]{1,0:T(2,128)(2,1)}, u32[]{:S(2)}) copy-start(bf16[2,1024]{1,0:T(2,128)(2,1)} %query_ref.1) | copy-start | bytes 12292
  4.5 0.7 %copy-start.4 = (s32[1,16]{1,0:T(1,128)S(1)}, s32[1,16]{1,0:T(1,128)}, u32[]{:S(2)}) copy-start(s32[1,16]{1,0:T(1,128)} %ids_ref.1) | copy-start | bytes 196
  5.1 0.7 %copy-start.5 = (s32[48]{0:T(128)S(1)}, s32[48]{0:T(128)}, u32[]{:S(2)}) copy-start(s32[48]{0:T(128)} %place_ref.1) | copy-start | bytes 580
  5.8 0.7 %copy-start.6 = (s32[48]{0:T(128)S(1)}, s32[48]{0:T(128)}, u32[]{:S(2)}) copy-start(s32[48]{0:T(128)} %count_ref.1) | copy-start | bytes 580

commit v2 on v1

--- a/solution.py
+++ b/solution.py
@@ -113,9 +113,9 @@
 
 
 def reader_kernel(
-    ids_ref,
-    place_ref,
-    count_ref,
+    ids_in,
+    place_in,
+    count_in,
     corpus_ref,
     query_ref,
     key_ref,
@@ -140,12 +140,15 @@
     c_send,
     c_recv,
     local_sem,
+    ids_ref,
+    place_ref,
+    count_ref,
 ):
     rows_here, length, width_in = corpus_ref.shape
     shard_rows, width = key_ref.shape
     half = shard_rows // 2
     heads = width // DH
-    per_question = ids_ref.shape[1]
+    per_question = ids_in.shape[1]
     group = lax.axis_index("groups")
     shard = lax.axis_index("passage")
     z = shard // 2
@@ -181,6 +184,13 @@
         query_ref, query_in.at[shard], local_sem.at[rows_here + 2]
     )
     own_query.start()
+    table_copies = []
+    for slot, (table, held) in enumerate(
+        ((ids_in, ids_ref), (place_in, place_ref), (count_in, count_ref))
+    ):
+        copy = pltpu.make_async_copy(table, held, local_sem.at[rows_here + 3 + slot])
+        copy.start()
+        table_copies.append(copy)
     pl.semaphore_wait(barrier, 8)
 
     def region(which, zz, xx, part):
@@ -279,6 +289,8 @@
     forward(1, 2)
     norm(5)
 
+    for copy in table_copies:
+        copy.wait()
     lengths = [jnp.int32(0) for _ in range(rows_here)]
     for number in range(per_question):
         name = ids_ref[0, number]
@@ -425,14 +437,13 @@
     rows_here, length, width_in = corpus.shape
     shard_rows, width = key_weight.shape
     lanes = width // DH * QT
-    smem = pl.BlockSpec(memory_space=pltpu.SMEM)
-    anywhere = pl.BlockSpec(memory_space=pl.ANY)
+    hbm = pl.BlockSpec(memory_space=pltpu.HBM)
     vmem = pl.BlockSpec(memory_space=pltpu.VMEM)
     dma = pltpu.SemaphoreType.DMA
     return pl.pallas_call(
         reader_kernel,
         out_shape=jax.ShapeDtypeStruct(queries.shape, jnp.bfloat16),
-        in_specs=[smem, smem, smem, anywhere, anywhere, anywhere, anywhere],
+        in_specs=[hbm] * 7,
         out_specs=vmem,
         scratch_shapes=[
             pltpu.VMEM(corpus.shape, jnp.bfloat16),
@@ -453,10 +464,13 @@
             dma((8,)),
             dma((8,)),
             dma((8,)),
-            dma((rows_here + 3,)),
+            dma((rows_here + 6,)),
+            pltpu.SMEM(retrieved.shape, jnp.int32),
+            pltpu.SMEM(placement_map.shape, jnp.int32),
+            pltpu.SMEM(valid_counts.shape, jnp.int32),
         ],
         compiler_params=pltpu.CompilerParams(
-            collective_id=0, has_side_effects=True, vmem_limit_bytes=48 * 1024 * 1024
+            collective_id=0, has_side_effects=True, vmem_limit_bytes=60 * 1024 * 1024
         ),
     )(retrieved, placement_map, valid_counts, corpus, queries, key_weight, value_weight)
 

time: 61.8 us -> 56.6 us (0.916)
  local copies, waits for them, and re-layouts: 7.03 us -> 1.28 us
  Pallas kernels: 54.5 us -> 55.2 us
    unnamed x15 -> x1, local copies, waits for them, and re-layouts: 7.03 us -> 1.28 us
    pallas_call x1, Pallas kernels: 54.5 us -> 55.2 us  [one_question(): pl.pallas_call(reader_kernel, out_shape=jax.ShapeDtypeStruct(queries.shap...]
where the time goes in v2:
time: 56.6 us; the launch traced here: 56.4 us
  Pallas kernels  55.2 us (98%)
  local copies, waits for them, and re-layouts  1.28 us (2%)
    pallas_call x1, Pallas kernels, one_question(): pl.pallas_call(reader_kernel, out_shape=jax.ShapeDtypeStruct(queries.shap...  55.2 us
    unnamed x1, local copies, waits for them, and re-layouts  1.28 us

profile of v2, /device:TPU:0, one launch (start us, length us, event | category | flops | bytes accessed | tf_op | source)
XLA Modules:
  0.0 56.4 jit_solution(17528713631814831079)
XLA Ops:
  0.0 55.2 %shard_map.73 = bf16[2,1024]{1,0:T(2,128)(2,1)} custom-call(s32[1,16]{1,0:T(1,128)} %ids_in.1, s32[48]{0:T(128)} %place_in.1, s32[48]{0:T(128)} %count_in.1, bf16[6,256,1024]{2,1,0:T(8,128)(2,1)} %corpus_ref.1, bf16[2,1024]{1,0:T(2,128)(2,1)} %query_ref.1, bf16[128,1024]{1,0:T(8,128)(2,1)} %key_ref.1, bf16[128,1024]{1,0:T(8,128)(2,1)} %value_ref.1), custom_call_target="tpu_custom_call" | custom-call | tf_op jit(solution)/shard_map/pallas_call | solution.py:443
  55.2 1.3 %copy.9 = bf16[2,1024]{1,0:T(2,128)(2,1)} copy(bf16[2,1024]{1,0:T(2,128)(2,1)} %shard_map.73) | data formatting | bytes 8192

commit v3 on v2

--- a/solution.py
+++ b/solution.py
@@ -222,6 +222,13 @@
         ).wait_recv()
 
     sent = []
+    for which, ref in ((0, key_ref), (1, value_ref)):
+        mine = ref.at[pl.ds(pl.multiple_of(group * half, half), half)]
+        send(which, 0, ref, region(which, z, x, None), {"passage": z1 * 2 + x})
+        send(which, 3, ref, region(which, z, x, None), at_x)
+        send(which, 1, mine, region(which, z, x, group), {"passage": z2 * 2 + x})
+        send(which, 2, mine, region(which, z, x, group), {"passage": z3 * 2 + x})
+
     for step in range(1, 8):
         peer = (shard + step) % 8
         copy = pltpu.make_async_remote_copy(
@@ -234,13 +241,6 @@
         )
         copy.start()
         sent.append(copy)
-
-    for which, ref in ((0, key_ref), (1, value_ref)):
-        mine = ref.at[pl.ds(pl.multiple_of(group * half, half), half)]
-        send(which, 0, ref, region(which, z, x, None), {"passage": z1 * 2 + x})
-        send(which, 3, ref, region(which, z, x, None), at_x)
-        send(which, 1, mine, region(which, z, x, group), {"passage": z2 * 2 + x})
-        send(which, 2, mine, region(which, z, x, group), {"passage": z3 * 2 + x})
 
     def forward(which, number):
         if number == 0:

time: 56.6 us -> 56.5 us (level)
  no operation moved by 1% of the time
where the time goes in v3:
time: 56.5 us; the launch traced here: 56.3 us
  Pallas kernels  55 us (97%)
  local copies, waits for them, and re-layouts  1.28 us (2%)
    pallas_call x1, Pallas kernels, one_question(): pl.pallas_call(reader_kernel, out_shape=jax.ShapeDtypeStruct(queries.shap...  55 us
    unnamed x1, local copies, waits for them, and re-layouts  1.28 us

profile of v3, /device:TPU:0, one launch (start us, length us, event | category | flops | bytes accessed | tf_op | source)
XLA Modules:
  0.0 56.3 jit_solution(12318324735214935338)
XLA Ops:
  0.0 55.0 %shard_map.73 = bf16[2,1024]{1,0:T(2,128)(2,1)} custom-call(s32[1,16]{1,0:T(1,128)} %ids_in.1, s32[48]{0:T(128)} %place_in.1, s32[48]{0:T(128)} %count_in.1, bf16[6,256,1024]{2,1,0:T(8,128)(2,1)} %corpus_ref.1, bf16[2,1024]{1,0:T(2,128)(2,1)} %query_ref.1, bf16[128,1024]{1,0:T(8,128)(2,1)} %key_ref.1, bf16[128,1024]{1,0:T(8,128)(2,1)} %value_ref.1), custom_call_target="tpu_custom_call" | custom-call | tf_op jit(solution)/shard_map/pallas_call | solution.py:443
  55.0 1.3 %copy.9 = bf16[2,1024]{1,0:T(2,128)(2,1)} copy(bf16[2,1024]{1,0:T(2,128)(2,1)} %shard_map.73) | data formatting | bytes 8192
